TPU v7x, 32 devices: a whole 2x2x4 slice. The times are simulated.
32 devices in a mesh: seq: 8 (over z, x), tp: 4 (over y, core).
Axes of the slice: x: 2, y: 2, z: 4, core: 2. Of those that a mesh axis runs over, the one named last changes fastest.
Arguments:
- draft_q: bfloat16 [256, 4096], P('seq', 'tp'), may hold values from -48 to 48
- draft_k: bfloat16 [256, 1024], P('seq', 'tp'), may hold values from -24 to 24
- draft_v: bfloat16 [256, 1024], P('seq', 'tp'), may hold values from -6 to 6
- cache_k: bfloat16 [4, 8192, 1024], P(None, 'seq', 'tp'), may hold values from -6 to 6
- cache_v: bfloat16 [4, 8192, 1024], P(None, 'seq', 'tp'), may hold values from -6 to 6
- lengths: int32 [4], replicated, may hold values from 2 to 8184, as said below
- migrating: int32 [4], replicated, may hold values from 0 to 1, as said below
- parents: int32 [4, 64], replicated, may hold values from -1 to 62, as said below
- accepted: int32 [4, 8], replicated, may hold values from -1 to 63, as said below
- out_weight: bfloat16 [4096, 4096], P('tp'), may hold values from -0.09375 to 0.09375
Outputs:
- attn_out: bfloat16 [256, 4096], P('seq', 'tp')
- new_k: bfloat16 [4, 8192, 1024], P(None, 'seq', 'tp')
- new_v: bfloat16 [4, 8192, 1024], P(None, 'seq', 'tp')
Inputs may be any that keep to these rules, and one draw needn't show every extreme that they name: `lengths`: some request has exactly 8184 valid positions. `migrating`: exactly 2 entries are 1. parents[r, 0] = -1 and 0 <= parents[r, i] < i for i >= 1. `accepted`: each row starts with node 0, each further entry's parent is the entry before it, 1 to 8 entries are nodes and the rest are -1; some row has 8 nodes.
All inputs are finite; a program needn't handle non-finite values.
Results may differ from a plain program's by a relative error of at most 0.015.
Values may be sent and summed in bfloat16 or wider, within the bound.
No kernel may reach another device: no remote copies, remote signals or barrier semaphores. Data moves between devices by JAX's collectives and lax.ppermute only.
A program may use at most 128 MiB of HBM per device.

v0:
```python
import math
import jax
import jax.numpy as jnp
from jax import lax
from jax.sharding import PartitionSpec as P

HD = 128


def joined(x, axis, combine):
    everything = jax.tree.map(
        lambda part, kind: lax.all_gather(part.astype(kind), axis),
        x,
        (jnp.bfloat16, jnp.bfloat16, jnp.bfloat16),
    )

    def take(k):
        return jax.tree.map(lambda part, own: part[k].astype(own.dtype), everything, x)

    return lax.fori_loop(
        1, lax.axis_size(axis), lambda k, so_far: combine(so_far, take(k)), take(0)
    )


def ancestry(parents):
    count = parents.shape[1]
    node = jnp.arange(count, dtype=jnp.int32)
    anc = (
        (node[None, :, None] == node[None, None, :]) | (parents[:, :, None] == node[None, None, :])
    ).astype(jnp.float32)
    for step in range(max(1, (count - 1).bit_length())):
        reach = jnp.einsum("rij,rjk->rik", anc, anc, precision=lax.Precision.HIGHEST)
        anc = jnp.where(anc + reach > 0.5, 1.0, 0.0).astype(jnp.float32)
    return anc


def combine(first, second):
    top_one, total_one, sum_one = first
    top_two, total_two, sum_two = second
    top = jnp.maximum(top_one, top_two)
    factor_one = jnp.exp(top_one - top)
    factor_two = jnp.exp(top_two - top)
    return (
        top,
        total_one * factor_one + total_two * factor_two,
        sum_one * factor_one[..., None] + sum_two * factor_two[..., None],
    )


def per_device(
    draft_q, draft_k, draft_v, cache_k, cache_v, lengths, migrating, parents, accepted, out_weight
):
    seq_count = lax.axis_size("seq")
    me_seq = lax.axis_index("seq")
    rows_dev, q_width = draft_q.shape
    requests, drafts = parents.shape
    cache_dev, kv_width = (cache_k.shape[1], cache_k.shape[2])
    kv_local = kv_width // HD
    group = q_width // kv_width
    heads_local = kv_local * group
    block = cache_dev // seq_count
    scale = 1.0 / math.sqrt(HD)
    accept_most = accepted.shape[1]
    q_all, k_all, v_all = (
        lax.all_gather(draft_q, "seq", axis=0, tiled=True),
        lax.all_gather(draft_k, "seq", axis=0, tiled=True),
        lax.all_gather(draft_v, "seq", axis=0, tiled=True),
    )
    order = jnp.argsort(1 - migrating, stable=True)[: requests // 2]
    half = requests // 2
    moved_k, moved_v = (
        lax.all_to_all(
            cache_k[order].reshape(half, seq_count, block, kv_width),
            "seq",
            split_axis=1,
            concat_axis=1,
            tiled=True,
        ),
        lax.all_to_all(
            cache_v[order].reshape(half, seq_count, block, kv_width),
            "seq",
            split_axis=1,
            concat_axis=1,
            tiled=True,
        ),
    )
    canon_k = cache_k.at[order].set(moved_k.reshape(half, cache_dev, kv_width))
    canon_v = cache_v.at[order].set(moved_v.reshape(half, cache_dev, kv_width))
    local = jnp.arange(cache_dev, dtype=jnp.int32)
    canon_pos = me_seq * cache_dev + local
    keys, values = (canon_k, canon_v)
    positions = jnp.broadcast_to(canon_pos[None, :], (requests, cache_dev))
    queries = q_all.reshape(requests, drafts, kv_local, group, HD)

    def partial_attend(operands):
        rows, key_rows, value_rows, live = operands
        scores = (
            jnp.einsum(
                "qkgd,pkd->kgqp",
                rows,
                key_rows.reshape(cache_dev, kv_local, HD),
                preferred_element_type=jnp.float32,
            )
            * scale
        )
        scores = jnp.where(live, scores, -1e30)
        top = jnp.max(scores, axis=-1)
        weights = jnp.where(live, jnp.exp(scores - top[..., None]), 0.0)
        total = jnp.sum(weights, axis=-1)
        summed = jnp.einsum(
            "kgqp,pkd->qkgd",
            weights.astype(jnp.bfloat16),
            value_rows.reshape(cache_dev, kv_local, HD),
            preferred_element_type=jnp.float32,
        )
        return (
            jnp.transpose(top, (2, 0, 1)).reshape(drafts, heads_local),
            jnp.transpose(total, (2, 0, 1)).reshape(drafts, heads_local),
            summed.reshape(drafts, heads_local, HD),
        )

    def nothing(operands):
        return (
            jnp.full((drafts, heads_local), -1e30, jnp.float32),
            jnp.zeros((drafts, heads_local), jnp.float32),
            jnp.zeros((drafts, heads_local, HD), jnp.float32),
        )

    tops, totals, sums = ([], [], [])
    for request in range(requests):
        live = positions[request] < lengths[request]
        top, total, summed = lax.cond(
            jnp.any(live),
            partial_attend,
            nothing,
            (queries[request], keys[request], values[request], live),
        )
        tops.append(top)
        totals.append(total)
        sums.append(summed)
    part_top = jnp.concatenate(tops, axis=0)
    part_total = jnp.concatenate(totals, axis=0)
    part_sum = jnp.concatenate(sums, axis=0)
    first_row = me_seq * rows_dev
    top_all, total_all, sum_all = joined((part_top, part_total, part_sum), "seq", combine)
    top = lax.dynamic_slice_in_dim(top_all, first_row, rows_dev, 0)
    total = lax.dynamic_slice_in_dim(total_all, first_row, rows_dev, 0)
    summed = lax.dynamic_slice_in_dim(sum_all, first_row, rows_dev, 0)
    anc = ancestry(parents).reshape(requests * drafts, drafts)
    anc_rows = lax.dynamic_slice_in_dim(anc, first_row, rows_dev, 0)
    mine = first_row + jnp.arange(rows_dev, dtype=jnp.int32)
    key_index = jnp.arange(requests * drafts, dtype=jnp.int32)
    allowed = (mine[:, None] // drafts == key_index[None, :] // drafts) & (
        jnp.tile(anc_rows, (1, requests)) > 0.5
    )
    own_q = draft_q.reshape(rows_dev, kv_local, group, HD)
    draft_scores = (
        jnp.einsum(
            "rkgd,nkd->rkgn",
            own_q,
            k_all.reshape(requests * drafts, kv_local, HD),
            preferred_element_type=jnp.float32,
        )
        * scale
    )
    draft_scores = jnp.where(allowed[:, None, None, :], draft_scores, -1e30)
    top = top.reshape(rows_dev, kv_local, group)
    new_top = jnp.maximum(top, jnp.max(draft_scores, axis=-1))
    keep = jnp.exp(top - new_top)
    draft_weights = jnp.where(
        allowed[:, None, None, :], jnp.exp(draft_scores - new_top[..., None]), 0.0
    )
    total = total.reshape(rows_dev, kv_local, group) * keep + jnp.sum(draft_weights, axis=-1)
    summed = summed.reshape(rows_dev, kv_local, group, HD) * keep[..., None]
    summed = summed + jnp.einsum(
        "rkgn,nkd->rkgd",
        draft_weights.astype(jnp.bfloat16),
        v_all.reshape(requests * drafts, kv_local, HD),
        preferred_element_type=jnp.float32,
    )
    attention = (summed / total[..., None]).astype(jnp.bfloat16).reshape(rows_dev, q_width)
    partial_out = jnp.dot(attention, out_weight, preferred_element_type=jnp.float32)
    attn_out = lax.psum_scatter(
        partial_out.astype(jnp.bfloat16), "tp", scatter_dimension=1, tiled=True
    )
    valid = accepted >= 0
    node = jnp.maximum(accepted, 0)
    slot = lengths[:, None] + jnp.arange(accept_most, dtype=jnp.int32)[None, :] - me_seq * cache_dev
    slot = jnp.where(valid & (slot >= 0) & (slot < cache_dev), slot, cache_dev)
    request_index = jnp.broadcast_to(jnp.arange(requests, dtype=jnp.int32)[:, None], slot.shape)
    rows_k = jnp.take_along_axis(k_all.reshape(requests, drafts, kv_width), node[..., None], axis=1)
    rows_v = jnp.take_along_axis(v_all.reshape(requests, drafts, kv_width), node[..., None], axis=1)
    new_k = canon_k.at[request_index, slot].set(rows_k, mode="drop")
    new_v = canon_v.at[request_index, slot].set(rows_v, mode="drop")
    return (attn_out, new_k, new_v)


def solution(mesh):
    in_specs = (
        P("seq", "tp"),
        P("seq", "tp"),
        P("seq", "tp"),
        P(None, "seq", "tp"),
        P(None, "seq", "tp"),
        P(),
        P(),
        P(),
        P(),
        P("tp", None),
    )
    out_specs = (P("seq", "tp"), P(None, "seq", "tp"), P(None, "seq", "tp"))
    return jax.shard_map(
        per_device, mesh=mesh, in_specs=in_specs, out_specs=out_specs, check_vma=False
    )
```

profile of v0, /device:TPU:0, one launch (start us, length us, event | category | flops | bytes accessed | tf_op | source)
XLA Modules:
  0.0 364.6 jit_solution(6048291003265357870)
XLA Ops:
  7.2 3.2 copy.235
  11.8 2.2 gather_fusion.1
  15.1 7.3 %all-to-all-start.1 = ((bf16[2,8,128,256]{3,2,0,1:T(8,128)(2,1)}), bf16[2,8,128,256]{3,2,0,1:T(8,128)(2,1)}, u32[]{:S(2)}, u32[]{:S(2)}) async-start(bf16[2,8,128,256]{3,2,0,1:T(8,128)(2,1)} %copy.105), calls=%async_computation.1 | async-start | bytes 2097152 | tf_op jit(solution)/shard_map/all_to_all | solution.py:79
  24.1 24.2 %all-to-all-done.1 = bf16[2,8,128,256]{3,2,0,1:T(8,128)(2,1)} async-done(((bf16[2,8,128,256]{3,2,0,1:T(8,128)(2,1)}), bf16[2,8,128,256]{3,2,0,1:T(8,128)(2,1)}, u32[]{:S(2)}, u32[]{:S(2)}) %all-to-all-start.1) | async-done | bytes 1048608 | tf_op jit(solution)/shard_map/all_to_all | solution.py:79
  48.2 3.6 all-to-all-start
  56.4 1.4 fusion.151
  63.0 38.2 %all_gather.21 = bf16[256,1024]{1,0:T(8,128)(2,1)} all-gather(bf16[32,1024]{1,0:T(8,128)(2,1)S(1)} %copy-done.12), channel_id=1, replica_groups=mesh['seq'=8,'tp'=4] {'seq'}, dimensions={0}, use_global_device_ids=true | all-gather | bytes 589824 | tf_op jit(solution)/shard_map/all_gather | solution.py:65
  101.2 2.4 copy.106
  103.6 3.1 scatter_fusion.1
  107.8 1.9 scatter_fusion
  109.7 13.5 %conditional.4 = (bf16[1,64,8]{1,2,0:T(8,128)(2,1)S(1)}, bf16[1,64,8]{1,2,0:T(8,128)(2,1)S(1)}, bf16[1,64,8,128]{3,2,1,0:T(8,128)(2,1)S(1)}) conditional(s32[]{:T(128)} %convert_element_type.117, () %tuple.87, (pred[1024]{0:T(1024)(128)(4,1)S(1)}, bf16[4,1024,256]{2,1,0:T(8,128)(2,1)S(1)}, bf16[256,1024]{1,0:T(8,128)(2,1)S(1)}, ...), branch_computations={%region_4.5_spmd, %region_5.8_spmd} | conditional | flops 275316224 | bytes 27276340 | solution.py:132
  109.7 2.4 copy.107
  113.3 1.8 bitcast_reduce_fusion
  115.1 4.0 %copy.108 = bf16[4,1024,256]{1,2,0:T(8,128)(2,1)} copy(bf16[4,1024,256]{2,1,0:T(8,128)(2,1)} %get-tuple-element.334) | data formatting | bytes 4194304 | tf_op jit(solution)/shard_map
  120.1 2.4 convolution_convert_fusion
  123.8 14.1 %conditional.5 = (bf16[1,64,8]{1,2,0:T(8,128)(2,1)S(1)}, bf16[1,64,8]{1,2,0:T(8,128)(2,1)}, bf16[1,64,8,128]{3,2,1,0:T(8,128)(2,1)S(1)}) conditional(s32[]{:T(128)} %convert_element_type.118, () %tuple.89, (pred[1024]{0:T(1024)(128)(4,1)S(1)}, bf16[4,1024,256]{2,1,0:T(8,128)(2,1)S(1)}, bf16[256,1024]{1,0:T(8,128)(2,1)S(1)}, ...), branch_computations={%region_9.10_spmd, %region_10.13_spmd} | conditional | flops 275316224 | bytes 27276340 | solution.py:132
  123.8 2.4 copy.109
  127.4 1.8 bitcast_reduce_fusion.1
  129.1 4.0 %copy.110 = bf16[4,1024,256]{1,2,0:T(8,128)(2,1)} copy(bf16[4,1024,256]{2,1,0:T(8,128)(2,1)} %get-tuple-element.338) | data formatting | bytes 4194304 | tf_op jit(solution)/shard_map
  134.2 2.4 convolution_convert_fusion.1
  138.5 14.1 %conditional.6 = (bf16[1,64,8]{1,2,0:T(8,128)(2,1)S(1)}, bf16[1,64,8]{1,2,0:T(8,128)(2,1)}, bf16[1,64,8,128]{3,2,1,0:T(8,128)(2,1)S(1)}) conditional(s32[]{:T(128)} %convert_element_type.119, () %tuple.91, (pred[1024]{0:T(1024)(128)(4,1)S(1)}, bf16[4,1024,256]{2,1,0:T(8,128)(2,1)S(1)}, bf16[256,1024]{1,0:T(8,128)(2,1)S(1)}, ...), branch_computations={%region_14.15_spmd, %region_15.18_spmd} | conditional | flops 275316224 | bytes 27276340 | solution.py:132
  138.5 2.4 copy.111
  142.1 1.8 bitcast_reduce_fusion.2
  143.8 4.0 %copy.112 = bf16[4,1024,256]{1,2,0:T(8,128)(2,1)} copy(bf16[4,1024,256]{2,1,0:T(8,128)(2,1)} %get-tuple-element.342) | data formatting | bytes 4194304 | tf_op jit(solution)/shard_map
  148.9 2.4 convolution_convert_fusion.2
  153.3 14.1 %conditional.7 = (bf16[1,64,8]{1,2,0:T(8,128)(2,1)S(1)}, bf16[1,64,8]{1,2,0:T(8,128)(2,1)}, bf16[1,64,8,128]{3,2,1,0:T(8,128)(2,1)S(1)}) conditional(s32[]{:T(128)} %convert_element_type.120, () %tuple.93, (pred[1024]{0:T(1024)(128)(4,1)S(1)}, bf16[4,1024,256]{2,1,0:T(8,128)(2,1)S(1)}, bf16[256,1024]{1,0:T(8,128)(2,1)S(1)}, ...), branch_computations={%region_19.20_spmd, %region_20.23_spmd} | conditional | flops 275316224 | bytes 27276340 | solution.py:132
  153.3 2.4 copy.113
  156.8 1.8 bitcast_reduce_fusion.3
  158.6 4.0 %copy.114 = bf16[4,1024,256]{1,2,0:T(8,128)(2,1)} copy(bf16[4,1024,256]{2,1,0:T(8,128)(2,1)} %get-tuple-element.346) | data formatting | bytes 4194304 | tf_op jit(solution)/shard_map
  163.6 2.4 convolution_convert_fusion.3
  167.3 1.8 pad_maximum_fusion
  172.8 31.0 %all_gather.25 = bf16[256,256]{1,0:T(8,128)(2,1)S(1)} all-gather(bf16[32,256]{1,0:T(8,128)(2,1)S(1)} %copy-done.14), channel_id=1, replica_groups=mesh['seq'=8,'tp'=4] {'seq'}, dimensions={0}, use_global_device_ids=true | all-gather | bytes 147456 | tf_op jit(solution)/shard_map/all_gather | solution.py:66
  204.0 31.6 %all_gather.26 = bf16[256,256]{1,0:T(8,128)(2,1)S(1)} all-gather(bf16[32,256]{1,0:T(8,128)(2,1)S(1)} %copy-done.15), channel_id=1, replica_groups=mesh['seq'=8,'tp'=4] {'seq'}, dimensions={0}, use_global_device_ids=true | all-gather | bytes 147456 | tf_op jit(solution)/shard_map/all_gather | solution.py:67
  236.4 1.5 fusion.155
  238.7 31.9 %all_gather.23 = bf16[8,256,8]{1,2,0:T(8,128)(2,1)} all-gather(bf16[1,256,8]{1,2,0:T(8,128)(2,1)S(1)} %pad_maximum_fusion.2), channel_id=1, replica_groups=mesh['seq'=8,'tp'=4] {'seq'}, dimensions={0}, use_global_device_ids=true | all-gather | bytes 36864 | tf_op jit(solution)/shard_map/all_gather | solution.py:12
  270.6 32.1 %all_gather.22 = bf16[8,256,8]{1,2,0:T(8,128)(2,1)} all-gather(bf16[1,256,8]{1,2,0:T(8,128)(2,1)S(1)} %pad_maximum_fusion.1), channel_id=1, replica_groups=mesh['seq'=8,'tp'=4] {'seq'}, dimensions={0}, use_global_device_ids=true | all-gather | bytes 36864 | tf_op jit(solution)/shard_map/all_gather | solution.py:12
  305.8 24.8 %while.19 = (s32[]{:T(128)}, f32[256,8]{0,1:T(8,128)}, f32[256,8]{0,1:T(8,128)S(1)}, f32[256,8,128]{2,1,0:T(8,128)S(1)}, bf16[8,256,8]{1,2,0:T(8,128)(2,1)}, /*i...) while((s32[]{:T(128)}, f32[256,8]{0,1:T(8,128)}, ...), condition=%wide.region_24.25_spmd, body=%wide.region_23.24_spmd.sunk | while | flops 1064965 | bytes 2728087 | solution.py:20
  307.4 1.9 fusion.173
  311.0 1.9 fusion.173
  314.5 1.9 fusion.173
  318.0 1.9 fusion.173
  321.6 1.9 fusion.173
  325.1 1.9 fusion.173
  328.6 1.9 fusion.173
  334.6 5.7 %convolution_convert_fusion.4 = bf16[32,4096]{1,0:T(8,128)(2,1)} fusion(bf16[32,1024]{1,0:T(8,128)(2,1)S(1)} %reshape.440, bf16[1024,4096]{1,0:T(8,128)(2,1)} %param.31), kind=kOutput, calls=%fused_computation.88 | convolution fusion | flops 268566528 | bytes 8716288 | tf_op jit(solution)/shard_map/dot_general | solution.py:182
  342.0 3.9 %scatter_fusion.3 = bf16[4,1024,256]{2,1,0:T(8,128)(2,1)} fusion(bf16[4,1024,256]{2,1,0:T(8,128)(2,1)} %scatter_fusion.1, s32[32]{0:T(128)S(1)} %reshape.505, bf16[32,256]{1,0:T(8,128)(2,1)S(1)} %get-tuple-element.381), kind=kCustom, calls=%fused_computation.7 | custom fusion | bytes 49408 | tf_op jit(solution)/shard_map/scatter | solution.py:194
  345.9 2.3 scatter_fusion.2
  348.2 9.5 %reduce-scatter.2.cloned.1.call-done = bf16[32,1024]{1,0:T(8,128)(2,1)} async-done(((bf16[32,4096]{1,0:T(8,128)(2,1)}), bf16[32,1024]{1,0:T(8,128)(2,1)}) %reduce-scatter.2.cloned.1.call-update) | async-done | bytes 65552 | tf_op jit(solution)/shard_map/reduce_scatter | solution.py:183
  (162 shorter events, 53.0 us)
Async XLA Ops:
  7.2 3.2 copy-start.6
  10.4 0.7 copy-start.23
  15.1 33.1 %all-to-all-start.1 = ((bf16[2,8,128,256]{3,2,0,1:T(8,128)(2,1)}), bf16[2,8,128,256]{3,2,0,1:T(8,128)(2,1)}, u32[]{:S(2)}, u32[]{:S(2)}) async-start(bf16[2,8,128,256]{3,2,0,1:T(8,128)(2,1)} %copy.105), calls=%async_computation.1 | async-start | bytes 2097152 | tf_op jit(solution)/shard_map/all_to_all | solution.py:79
  23.0 28.9 %copy-start.16 = (s32[4]{0:T(128)S(1)}, s32[4]{0:T(128)}, u32[]{:S(2)}) copy-start(s32[4]{0:T(128)} %param.27) | copy-start | bytes 52
  23.0 40.0 %copy-start.12 = (bf16[32,1024]{1,0:T(8,128)(2,1)S(1)}, bf16[32,1024]{1,0:T(8,128)(2,1)}, u32[]{:S(2)}) copy-start(bf16[32,1024]{1,0:T(8,128)(2,1)} %param.22) | copy-start | bytes 196612
  48.2 58.5 %all-to-all-start = ((bf16[2,8,128,256]{3,2,0,1:T(8,128)(2,1)}), bf16[2,8,128,256]{3,2,0,1:T(8,128)(2,1)S(1)}, u32[]{:S(2)}, u32[]{:S(2)}) async-start(bf16[2,8,128,256]{3,2,0,1:T(8,128)(2,1)} %copy.103), calls=%async_computation | async-start | bytes 2097152 | tf_op jit(solution)/shard_map/all_to_all | solution.py:72
  51.8 252.9 %all-gather.2.cloned.1.call-start = ((), (), s32[]{:S(2)}) async-start(), calls=%async_computation.3 | async-start | bytes 4718592 | tf_op jit(solution)/shard_map/all_gather | solution.py:12
  107.8 1.9 copy-start.5
  120.1 2.5 copy-start.1
  123.2 0.6 copy-start.19
  123.2 0.6 copy-start.21
  134.2 2.5 copy-start.2
  137.9 0.7 copy-start.9
  148.9 2.5 copy-start.3
  152.6 0.6 copy-start.11
  152.6 14.7 %copy-start.10 = (bf16[1,64,8,128]{3,2,1,0:T(8,128)(2,1)S(1)}, bf16[1,64,8,128]{3,2,1,0:T(8,128)(2,1)}, u32[]{:S(2)}) copy-start(bf16[1,64,8,128]{3,2,1,0:T(8,128)(2,1)} %copy-done.9) | copy-start | bytes 393220
  163.6 2.5 copy-start.4
  167.3 5.5 %copy-start.14 = (bf16[32,256]{1,0:T(8,128)(2,1)S(1)}, bf16[32,256]{1,0:T(8,128)(2,1)}, u32[]{:S(2)}) copy-start(bf16[32,256]{1,0:T(8,128)(2,1)} %param.23) | copy-start | bytes 49156
  167.3 36.6 %copy-start.15 = (bf16[32,256]{1,0:T(8,128)(2,1)S(1)}, bf16[32,256]{1,0:T(8,128)(2,1)}, u32[]{:S(2)}) copy-start(bf16[32,256]{1,0:T(8,128)(2,1)} %param.24) | copy-start | bytes 49156
  169.1 68.8 %copy-start.22 = (bf16[1,64,8]{1,2,0:T(8,128)(2,1)S(1)}, bf16[1,64,8]{1,2,0:T(8,128)(2,1)}, u32[]{:S(2)}) copy-start(bf16[1,64,8]{1,2,0:T(8,128)(2,1)} %copy-done.21) | copy-start | bytes 3076
  169.1 101.4 %copy-start.20 = (bf16[1,64,8]{1,2,0:T(8,128)(2,1)S(1)}, bf16[1,64,8]{1,2,0:T(8,128)(2,1)}, u32[]{:S(2)}) copy-start(bf16[1,64,8]{1,2,0:T(8,128)(2,1)} %copy-done.19) | copy-start | bytes 3076
  169.1 188.6 %reduce-scatter.2.cloned.1.call-start = ((), (), s32[]{:S(2)}) async-start(), calls=%async_computation.4 | async-start | bytes 327680 | tf_op jit(solution)/shard_map/reduce_scatter | solution.py:183
  235.6 69.1 %copy-start.7 = (bf16[256,256]{1,0:T(8,128)(2,1)}, bf16[256,256]{1,0:T(8,128)(2,1)S(1)}, u32[]{:S(2)}) copy-start(bf16[256,256]{1,0:T(8,128)(2,1)S(1)} %all_gather.26) | copy-start | bytes 393220
  236.4 68.3 %copy-start.13 = (pred[32,256]{1,0:T(8,128)(4,1)}, pred[32,256]{1,0:T(8,128)(4,1)S(1)}, u32[]{:S(2)}) copy-start(pred[32,256]{1,0:T(8,128)(4,1)S(1)} %compare_and_fusion) | copy-start | bytes 24580
  334.6 5.7 %copy-start.17 = (s32[4]{0:T(128)S(1)}, s32[4]{0:T(128)}, u32[]{:S(2)}) copy-start(s32[4]{0:T(128)} %param.27) | copy-start | bytes 52
  334.6 5.7 %copy-start.18 = (s32[4,8]{1,0:T(4,128)S(1)}, s32[4,8]{1,0:T(4,128)}, u32[]{:S(2)}) copy-start(s32[4,8]{1,0:T(4,128)} %param.30) | copy-start | bytes 388
  334.6 6.6 %copy-start.8 = (bf16[256,256]{1,0:T(8,128)(2,1)S(1)}, bf16[256,256]{1,0:T(8,128)(2,1)}, u32[]{:S(2)}) copy-start(bf16[256,256]{1,0:T(8,128)(2,1)} %copy-done.7) | copy-start | bytes 393220
  348.2 9.6 %copy-start = (bf16[4,1024,256]{2,1,0:T(8,128)(2,1)}, bf16[4,1024,256]{2,1,0:T(8,128)(2,1)S(1)}, u32[]{:S(2)}) copy-start(bf16[4,1024,256]{2,1,0:T(8,128)(2,1)S(1)} %scatter_fusion.2) | copy-start | bytes 6291460
Sparse Core Ops, SparseCore 0:
  169.3 73.3 all-gather.1
  340.4 17.2 reduce-scatter.1
where the time goes:
time: 367 us; the launch traced here: 365 us
  blocking collectives  165 us (45%)
  local copies, waits for them, and re-layouts  66.7 us (18%)
  other arithmetic  43.6 us (12%)
  waiting for transfers between devices  33.8 us (9%)
  matrix products  27.2 us (7%)
  between operations  17 us (5%)
  starting transfers between devices  10.9 us (3%)
    all_gather x2, blocking collectives, joined(): lax.all_gather(part.astype(kind), axis)  64 us
    all_gather x1, blocking collectives, per_device(): lax.all_gather(draft_q, 'seq', axis=0, tiled=True)  38.2 us
    all_gather x1, blocking collectives, per_device(): lax.all_gather(draft_v, 'seq', axis=0, tiled=True)  31.6 us
    all_gather x1, blocking collectives, per_device(): lax.all_gather(draft_k, 'seq', axis=0, tiled=True)  31 us
    another operation x8, local copies, waits for them, and re-layouts  25.4 us
    all_to_all x1, waiting for transfers between devices, per_device(): lax.all_to_all(cache_v[order].reshape(half, seq_count, block, kv_width),...  24.2 us
    add x7, other arithmetic, combine(): sum_one * factor_one[..., None] + sum_two * factor_two[..., None]  13.5 us
    reduce_scatter x1, waiting for transfers between devices, per_device(): lax.psum_scatter(partial_out.astype(jnp.bfloat16), 'tp', scatter_dimensio...  9.54 us
  transfers between devices with their start and end apart: 4, of which 2 were waited for; matrix products, arithmetic and copies ran while one was open for 9% of the time, Pallas kernels for 0%

commit v1 on v0

--- a/solution.py
+++ b/solution.py
@@ -50,6 +50,26 @@
 def per_device(
     draft_q, draft_k, draft_v, cache_k, cache_v, lengths, migrating, parents, accepted, out_weight
 ):
+
+    def deliver_records(t0):
+        arr_out, y1, part_now = (lax.axis_size("seq"), lax.axis_index("seq"), t0.shape[0])
+        side_arr, x_next = (t0, 1)
+        while x_next < arr_out:
+            side_arr = jnp.concatenate(
+                [
+                    side_arr,
+                    lax.ppermute(
+                        side_arr,
+                        "seq",
+                        list(map(lambda nth: (nth, (nth - x_next) % arr_out), range(arr_out))),
+                    ),
+                ],
+                axis=0,
+            )
+            x_next = 2 * x_next
+        after = jnp.roll(side_arr, y1 * part_now, axis=0)
+        return after
+
     seq_count = lax.axis_size("seq")
     me_seq = lax.axis_index("seq")
     rows_dev, q_width = draft_q.shape
@@ -62,7 +82,7 @@
     scale = 1.0 / math.sqrt(HD)
     accept_most = accepted.shape[1]
     q_all, k_all, v_all = (
-        lax.all_gather(draft_q, "seq", axis=0, tiled=True),
+        deliver_records(draft_q),
         lax.all_gather(draft_k, "seq", axis=0, tiled=True),
         lax.all_gather(draft_v, "seq", axis=0, tiled=True),
     )

time: 367 us -> 365 us (level)
  blocking collectives: 165 us -> 127 us
  starting transfers between devices: 10.9 us -> 27.8 us
  waiting for transfers between devices: 33.8 us -> 44.8 us
  local copies, waits for them, and re-layouts: 66.7 us -> 76.7 us
    all_gather x1 -> x0, blocking collectives: 38.2 us -> none  [per_device(): lax.all_gather(draft_q, 'seq', axis=0, tiled=True)]
    ppermute x0 -> x3, starting transfers between devices: none -> 16.9 us  [deliver_records(): lax.ppermute(side_arr, 'seq', list(map(lambda nth: (nth, (nth - x_next) %...]
    ppermute x0 -> x3, waiting for transfers between devices: none -> 14 us  [deliver_records(): lax.ppermute(side_arr, 'seq', list(map(lambda nth: (nth, (nth - x_next) %...]
    unnamed x42 -> x51, local copies, waits for them, and re-layouts: 5.79 us -> 11.1 us
    all_to_all x1, waiting for transfers between devices: 24.2 us -> 20.2 us  [per_device(): lax.all_to_all(cache_v[order].reshape(half, seq_count, block, kv_width),...]
  transfers between devices with their start and end apart: 4 -> 7, of which waited for: 2 -> 4; matrix products, arithmetic and copies ran while one was open for 9% -> 11% of each run, Pallas kernels for 0% -> 0%
where the time goes in v1:
time: 365 us; the launch traced here: 362 us
  blocking collectives  127 us (35%)
  local copies, waits for them, and re-layouts  76.7 us (21%)
  waiting for transfers between devices  44.8 us (12%)
  other arithmetic  42.3 us (12%)
  starting transfers between devices  27.8 us (8%)
  matrix products  26.4 us (7%)
  between operations  17.2 us (5%)
    all_gather x2, blocking collectives, joined(): lax.all_gather(part.astype(kind), axis)  64 us
    all_gather x1, blocking collectives, per_device(): lax.all_gather(draft_v, 'seq', axis=0, tiled=True)  31.6 us
    all_gather x1, blocking collectives, per_device(): lax.all_gather(draft_k, 'seq', axis=0, tiled=True)  31 us
    another operation x8, local copies, waits for them, and re-layouts  25.4 us
    all_to_all x1, waiting for transfers between devices, per_device(): lax.all_to_all(cache_v[order].reshape(half, seq_count, block, kv_width),...  20.2 us
    ppermute x3, starting transfers between devices, deliver_records(): lax.ppermute(side_arr, 'seq', list(map(lambda nth: (nth, (nth - x_next) %...  16.9 us
    ppermute x3, waiting for transfers between devices, deliver_records(): lax.ppermute(side_arr, 'seq', list(map(lambda nth: (nth, (nth - x_next) %...  14 us
    add x7, other arithmetic, combine(): sum_one * factor_one[..., None] + sum_two * factor_two[..., None]  13.5 us
  transfers between devices with their start and end apart: 7, of which 4 were waited for; matrix products, arithmetic and copies ran while one was open for 11% of the time, Pallas kernels for 0%

profile of v1, /device:TPU:0, one launch (start us, length us, event | category | flops | bytes accessed | tf_op | source)
XLA Modules:
  0.0 362.4 jit_solution(9239591999696082979)
XLA Ops:
  7.2 3.2 copy.242
  11.8 2.2 gather_fusion.1
  15.1 7.3 %all-to-all-start.1 = ((bf16[2,8,128,256]{3,2,0,1:T(8,128)(2,1)}), bf16[2,8,128,256]{3,2,0,1:T(8,128)(2,1)}, u32[]{:S(2)}, u32[]{:S(2)}) async-start(bf16[2,8,128,256]{3,2,0,1:T(8,128)(2,1)} %copy.105), calls=%async_computation.1 | async-start | bytes 2097152 | tf_op jit(solution)/shard_map/all_to_all | solution.py:99
  22.4 4.7 %collective-permute-start = (bf16[32,1024]{1,0:T(8,128)(2,1)S(1)}, bf16[32,1024]{1,0:T(8,128)(2,1)S(1)}, u32[]{:S(2)}, u32[]{:S(2)}) collective-permute-start(bf16[32,1024]{1,0:T(8,128)(2,1)S(1)} %copy-done.7), channel_id=1, source_target_pairs={{0,28},{4,0},{8,4},{12,8},{16,12},{20,16},{24,20},{28,24},{1,29},{... | collective-permute-start | bytes 196616 | tf_op jit(solution)/shard_map/ppermute | solution.py:61
  28.8 20.2 %all-to-all-done.1 = bf16[2,8,128,256]{3,2,0,1:T(8,128)(2,1)} async-done(((bf16[2,8,128,256]{3,2,0,1:T(8,128)(2,1)}), bf16[2,8,128,256]{3,2,0,1:T(8,128)(2,1)}, u32[]{:S(2)}, u32[]{:S(2)}) %all-to-all-start.1) | async-done | bytes 1048608 | tf_op jit(solution)/shard_map/all_to_all | solution.py:99
  49.0 3.6 all-to-all-start
  54.5 3.8 %collective-permute-start.1 = (bf16[64,1024]{1,0:T(8,128)(2,1)S(1)}, bf16[64,1024]{1,0:T(8,128)(2,1)S(1)}, u32[]{:S(2)}, u32[]{:S(2)}) collective-permute-start(bf16[64,1024]{1,0:T(8,128)(2,1)S(1)} %pad_maximum_fusion.2), channel_id=1, source_target_pairs={{0,24},{4,28},{8,0},{12,4},{16,8},{20,12},{24,16},{28,20},{1,25},{... | collective-permute-start | bytes 393224 | tf_op jit(solution)/shard_map/ppermute | solution.py:61
  59.5 12.6 %collective-permute-done.1 = bf16[64,1024]{1,0:T(8,128)(2,1)S(1)} collective-permute-done((bf16[64,1024]{1,0:T(8,128)(2,1)S(1)}, bf16[64,1024]{1,0:T(8,128)(2,1)S(1)}, u32[]{:S(2)}, u32[]{:S(2)}) %collective-permute-start.1) | collective-permute-done | bytes 131104 | tf_op jit(solution)/shard_map/ppermute | solution.py:61
  72.8 8.4 %collective-permute-start.2 = (bf16[128,1024]{1,0:T(8,128)(2,1)}, bf16[128,1024]{1,0:T(8,128)(2,1)}, u32[]{:S(2)}, u32[]{:S(2)}) collective-permute-start(bf16[128,1024]{1,0:T(8,128)(2,1)} %pad_maximum_fusion.1), channel_id=1, source_target_pairs={{0,16},{4,20},{8,24},{12,28},{16,0},{20,4},{24,8},{28,12},{1,17},{... | collective-permute-start | bytes 786440 | tf_op jit(solution)/shard_map/ppermute | solution.py:61
  97.5 1.9 constant_dynamic-slice_fusion.3
  99.4 2.4 copy.106
  101.8 3.1 scatter_fusion.1
  105.9 1.9 scatter_fusion
  107.9 14.2 %conditional.4 = (bf16[1,64,8]{1,2,0:T(8,128)(2,1)S(1)}, bf16[1,64,8]{1,2,0:T(8,128)(2,1)S(1)}, bf16[1,64,8,128]{3,2,1,0:T(8,128)(2,1)}) conditional(s32[]{:T(128)} %convert_element_type.117, () %tuple.87, (pred[1024]{0:T(1024)(128)(4,1)S(1)}, bf16[4,1024,256]{2,1,0:T(8,128)(2,1)S(1)}, bf16[256,1024]{1,0:T(8,128)(2,1)S(1)}, ...), branch_computations={%region_4.5_spmd, %region_5.8_spmd} | conditional | flops 275316224 | bytes 27276340 | solution.py:152
  107.9 2.4 copy.107
  111.5 1.8 bitcast_reduce_fusion
  113.2 4.0 %copy.108 = bf16[4,1024,256]{1,2,0:T(8,128)(2,1)} copy(bf16[4,1024,256]{2,1,0:T(8,128)(2,1)} %get-tuple-element.334) | data formatting | bytes 4194304 | tf_op jit(solution)/shard_map
  118.3 2.4 convolution_convert_fusion
  122.6 14.1 %conditional.5 = (bf16[1,64,8]{1,2,0:T(8,128)(2,1)S(1)}, bf16[1,64,8]{1,2,0:T(8,128)(2,1)S(1)}, bf16[1,64,8,128]{3,2,1,0:T(8,128)(2,1)}) conditional(s32[]{:T(128)} %convert_element_type.118, () %tuple.89, (pred[1024]{0:T(1024)(128)(4,1)S(1)}, bf16[4,1024,256]{2,1,0:T(8,128)(2,1)S(1)}, bf16[256,1024]{1,0:T(8,128)(2,1)S(1)}, ...), branch_computations={%region_9.10_spmd, %region_10.13_spmd} | conditional | flops 275316224 | bytes 27276340 | solution.py:152
  122.6 2.4 copy.109
  126.1 1.8 bitcast_reduce_fusion.1
  127.9 4.0 %copy.110 = bf16[4,1024,256]{1,2,0:T(8,128)(2,1)} copy(bf16[4,1024,256]{2,1,0:T(8,128)(2,1)} %get-tuple-element.338) | data formatting | bytes 4194304 | tf_op jit(solution)/shard_map
  133.0 2.4 convolution_convert_fusion.1
  137.3 14.1 %conditional.6 = (bf16[1,64,8]{1,2,0:T(8,128)(2,1)S(1)}, bf16[1,64,8]{1,2,0:T(8,128)(2,1)S(1)}, bf16[1,64,8,128]{3,2,1,0:T(8,128)(2,1)}) conditional(s32[]{:T(128)} %convert_element_type.119, () %tuple.91, (pred[1024]{0:T(1024)(128)(4,1)S(1)}, bf16[4,1024,256]{2,1,0:T(8,128)(2,1)S(1)}, bf16[256,1024]{1,0:T(8,128)(2,1)S(1)}, ...), branch_computations={%region_14.15_spmd, %region_15.18_spmd} | conditional | flops 275316224 | bytes 27276340 | solution.py:152
  137.3 2.4 copy.111
  142.6 4.0 %copy.112 = bf16[4,1024,256]{1,2,0:T(8,128)(2,1)} copy(bf16[4,1024,256]{2,1,0:T(8,128)(2,1)} %get-tuple-element.342) | data formatting | bytes 4194304 | tf_op jit(solution)/shard_map
  147.7 2.4 convolution_convert_fusion.2
  152.0 13.5 %conditional.7 = (bf16[1,64,8]{1,2,0:T(8,128)(2,1)S(1)}, bf16[1,64,8]{1,2,0:T(8,128)(2,1)S(1)}, bf16[1,64,8,128]{3,2,1,0:T(8,128)(2,1)S(1)}) conditional(s32[]{:T(128)} %convert_element_type.120, () %tuple.93, (pred[1024]{0:T(1024)(128)(4,1)S(1)}, bf16[4,1024,256]{2,1,0:T(8,128)(2,1)S(1)}, bf16[256,1024]{1,0:T(8,128)(2,1)S(1)}, ...), branch_computations={%region_19.20_spmd, %region_20.23_spmd} | conditional | flops 275316224 | bytes 27276340 | solution.py:152
  152.0 2.4 copy.113
  157.3 4.0 %copy.114 = bf16[4,1024,256]{1,2,0:T(8,128)(2,1)} copy(bf16[4,1024,256]{2,1,0:T(8,128)(2,1)} %get-tuple-element.346) | data formatting | bytes 4194304 | tf_op jit(solution)/shard_map
  162.4 2.4 convolution_convert_fusion.3
  165.6 1.9 pad_maximum_fusion
  169.5 31.0 %all_gather.21 = bf16[256,256]{1,0:T(8,128)(2,1)S(1)} all-gather(bf16[32,256]{1,0:T(8,128)(2,1)S(1)} %copy-done.11), channel_id=1, replica_groups=mesh['seq'=8,'tp'=4] {'seq'}, dimensions={0}, use_global_device_ids=true | all-gather | bytes 147456 | tf_op jit(solution)/shard_map/all_gather | solution.py:86
  200.7 31.6 %all_gather.22 = bf16[256,256]{1,0:T(8,128)(2,1)S(1)} all-gather(bf16[32,256]{1,0:T(8,128)(2,1)S(1)} %copy-done.12), channel_id=1, replica_groups=mesh['seq'=8,'tp'=4] {'seq'}, dimensions={0}, use_global_device_ids=true | all-gather | bytes 147456 | tf_op jit(solution)/shard_map/all_gather | solution.py:87
  235.4 32.1 %all_gather.19 = bf16[8,256,8]{1,2,0:T(8,128)(2,1)} all-gather(bf16[1,256,8]{1,2,0:T(8,128)(2,1)S(1)} %pad_maximum_fusion.4), channel_id=1, replica_groups=mesh['seq'=8,'tp'=4] {'seq'}, dimensions={0}, use_global_device_ids=true | all-gather | bytes 36864 | tf_op jit(solution)/shard_map/all_gather | solution.py:12
  267.6 31.9 %all_gather.18 = bf16[8,256,8]{1,2,0:T(8,128)(2,1)} all-gather(bf16[1,256,8]{1,2,0:T(8,128)(2,1)S(1)} %pad_maximum_fusion.3), channel_id=1, replica_groups=mesh['seq'=8,'tp'=4] {'seq'}, dimensions={0}, use_global_device_ids=true | all-gather | bytes 36864 | tf_op jit(solution)/shard_map/all_gather | solution.py:12
  302.6 24.8 %while.19 = (s32[]{:T(128)}, f32[256,8]{0,1:T(8,128)}, f32[256,8]{0,1:T(8,128)S(1)}, f32[256,8,128]{2,1,0:T(8,128)S(1)}, bf16[8,256,8]{1,2,0:T(8,128)(2,1)}, /*i...) while((s32[]{:T(128)}, f32[256,8]{0,1:T(8,128)}, ...), condition=%wide.region_24.25_spmd, body=%wide.region_23.24_spmd.sunk | while | flops 1064965 | bytes 2728087 | solution.py:20
  304.2 1.9 fusion.173
  307.7 1.9 fusion.173
  311.3 1.9 fusion.173
  314.8 1.9 fusion.173
  318.3 1.9 fusion.173
  321.9 1.9 fusion.173
  325.4 1.9 fusion.173
  331.4 5.7 %convolution_convert_fusion.4 = bf16[32,4096]{1,0:T(8,128)(2,1)} fusion(bf16[32,1024]{1,0:T(8,128)(2,1)S(1)} %reshape.440, bf16[1024,4096]{1,0:T(8,128)(2,1)} %param.31), kind=kOutput, calls=%fused_computation.88 | convolution fusion | flops 268566528 | bytes 8716288 | tf_op jit(solution)/shard_map/dot_general | solution.py:202
  338.8 3.9 %scatter_fusion.3 = bf16[4,1024,256]{2,1,0:T(8,128)(2,1)} fusion(bf16[4,1024,256]{2,1,0:T(8,128)(2,1)} %scatter_fusion.1, s32[32]{0:T(128)S(1)} %reshape.505, bf16[32,256]{1,0:T(8,128)(2,1)S(1)} %get-tuple-element.381), kind=kCustom, calls=%fused_computation.7 | custom fusion | bytes 49408 | tf_op jit(solution)/shard_map/scatter | solution.py:214
  342.7 2.3 scatter_fusion.2
  345.0 10.6 %reduce-scatter.2.cloned.1.call-done = bf16[32,1024]{1,0:T(8,128)(2,1)} async-done(((bf16[32,4096]{1,0:T(8,128)(2,1)}), bf16[32,1024]{1,0:T(8,128)(2,1)}) %reduce-scatter.2.cloned.1.call-update) | async-done | bytes 65552 | tf_op jit(solution)/shard_map/reduce_scatter | solution.py:203
  (180 shorter events, 66.8 us)
Async XLA Ops:
  7.2 3.2 copy-start.5
  10.4 0.7 copy-start.24
  14.0 8.4 %copy-start.7 = (bf16[32,1024]{1,0:T(8,128)(2,1)S(1)}, bf16[32,1024]{1,0:T(8,128)(2,1)}, u32[]{:S(2)}) copy-start(bf16[32,1024]{1,0:T(8,128)(2,1)} %param.22) | copy-start | bytes 196612
  15.1 33.8 %all-to-all-start.1 = ((bf16[2,8,128,256]{3,2,0,1:T(8,128)(2,1)}), bf16[2,8,128,256]{3,2,0,1:T(8,128)(2,1)}, u32[]{:S(2)}, u32[]{:S(2)}) async-start(bf16[2,8,128,256]{3,2,0,1:T(8,128)(2,1)} %copy.105), calls=%async_computation.1 | async-start | bytes 2097152 | tf_op jit(solution)/shard_map/all_to_all | solution.py:99
  22.4 32.1 %collective-permute-start = (bf16[32,1024]{1,0:T(8,128)(2,1)S(1)}, bf16[32,1024]{1,0:T(8,128)(2,1)S(1)}, u32[]{:S(2)}, u32[]{:S(2)}) collective-permute-start(bf16[32,1024]{1,0:T(8,128)(2,1)S(1)} %copy-done.7), channel_id=1, source_target_pairs={{0,28},{4,0},{8,4},{12,8},{16,12},{20,16},{24,20},{28,24},{1,29},{... | collective-permute-start | bytes 196616 | tf_op jit(solution)/shard_map/ppermute | solution.py:61
  27.7 24.8 %copy-start.13 = (s32[4]{0:T(128)S(1)}, s32[4]{0:T(128)}, u32[]{:S(2)}) copy-start(s32[4]{0:T(128)} %param.27) | copy-start | bytes 52
  49.0 55.9 %all-to-all-start = ((bf16[2,8,128,256]{3,2,0,1:T(8,128)(2,1)}), bf16[2,8,128,256]{3,2,0,1:T(8,128)(2,1)S(1)}, u32[]{:S(2)}, u32[]{:S(2)}) async-start(bf16[2,8,128,256]{3,2,0,1:T(8,128)(2,1)} %copy.103), calls=%async_computation | async-start | bytes 2097152 | tf_op jit(solution)/shard_map/all_to_all | solution.py:92
  52.5 248.9 %all-gather.2.cloned.1.call-start = ((), (), s32[]{:S(2)}) async-start(), calls=%async_computation.3 | async-start | bytes 4718592 | tf_op jit(solution)/shard_map/all_gather | solution.py:12
  54.5 17.6 %collective-permute-start.1 = (bf16[64,1024]{1,0:T(8,128)(2,1)S(1)}, bf16[64,1024]{1,0:T(8,128)(2,1)S(1)}, u32[]{:S(2)}, u32[]{:S(2)}) collective-permute-start(bf16[64,1024]{1,0:T(8,128)(2,1)S(1)} %pad_maximum_fusion.2), channel_id=1, source_target_pairs={{0,24},{4,28},{8,0},{12,4},{16,8},{20,12},{24,16},{28,20},{1,25},{... | collective-permute-start | bytes 393224 | tf_op jit(solution)/shard_map/ppermute | solution.py:61
  72.8 19.5 %collective-permute-start.2 = (bf16[128,1024]{1,0:T(8,128)(2,1)}, bf16[128,1024]{1,0:T(8,128)(2,1)}, u32[]{:S(2)}, u32[]{:S(2)}) collective-permute-start(bf16[128,1024]{1,0:T(8,128)(2,1)} %pad_maximum_fusion.1), channel_id=1, source_target_pairs={{0,16},{4,20},{8,24},{12,28},{16,0},{20,4},{24,8},{28,12},{1,17},{... | collective-permute-start | bytes 786440 | tf_op jit(solution)/shard_map/ppermute | solution.py:61
  105.9 1.9 copy-start.6
  118.3 3.1 copy-start.1
  122.0 0.6 copy-start.16
  133.0 3.1 copy-start.2
  136.7 0.6 copy-start.18
  147.7 3.1 copy-start.3
  151.4 0.6 copy-start.20
  151.4 16.2 %copy-start.23 = (s32[4,64]{1,0:T(4,128)S(1)}, s32[4,64]{1,0:T(4,128)}, u32[]{:S(2)}) copy-start(s32[4,64]{1,0:T(4,128)} %param.29) | copy-start | bytes 3076
  162.4 2.5 copy-start.4
  165.5 3.9 %copy-start.22 = (bf16[1,64,8]{1,2,0:T(8,128)(2,1)}, bf16[1,64,8]{1,2,0:T(8,128)(2,1)S(1)}, u32[]{:S(2)}) copy-start(bf16[1,64,8]{1,2,0:T(8,128)(2,1)S(1)} %get-tuple-element.297) | copy-start | bytes 3076
  165.5 4.0 %copy-start.11 = (bf16[32,256]{1,0:T(8,128)(2,1)S(1)}, bf16[32,256]{1,0:T(8,128)(2,1)}, u32[]{:S(2)}) copy-start(bf16[32,256]{1,0:T(8,128)(2,1)} %param.23) | copy-start | bytes 49156
  165.5 35.1 %copy-start.12 = (bf16[32,256]{1,0:T(8,128)(2,1)S(1)}, bf16[32,256]{1,0:T(8,128)(2,1)}, u32[]{:S(2)}) copy-start(bf16[32,256]{1,0:T(8,128)(2,1)} %param.24) | copy-start | bytes 49156
  167.5 67.2 %copy-start.17 = (bf16[1,64,8]{1,2,0:T(8,128)(2,1)S(1)}, bf16[1,64,8]{1,2,0:T(8,128)(2,1)}, u32[]{:S(2)}) copy-start(bf16[1,64,8]{1,2,0:T(8,128)(2,1)} %copy-done.16) | copy-start | bytes 3076
  167.5 67.2 %copy-start.19 = (bf16[1,64,8]{1,2,0:T(8,128)(2,1)S(1)}, bf16[1,64,8]{1,2,0:T(8,128)(2,1)}, u32[]{:S(2)}) copy-start(bf16[1,64,8]{1,2,0:T(8,128)(2,1)} %copy-done.18) | copy-start | bytes 3076
  167.5 67.2 %copy-start.21 = (bf16[1,64,8]{1,2,0:T(8,128)(2,1)S(1)}, bf16[1,64,8]{1,2,0:T(8,128)(2,1)}, u32[]{:S(2)}) copy-start(bf16[1,64,8]{1,2,0:T(8,128)(2,1)} %copy-done.20) | copy-start | bytes 3076
  167.5 188.1 %reduce-scatter.2.cloned.1.call-start = ((), (), s32[]{:S(2)}) async-start(), calls=%async_computation.4 | async-start | bytes 327680 | tf_op jit(solution)/shard_map/reduce_scatter | solution.py:203
  232.3 69.1 %copy-start.8 = (bf16[256,256]{1,0:T(8,128)(2,1)}, bf16[256,256]{1,0:T(8,128)(2,1)S(1)}, u32[]{:S(2)}) copy-start(bf16[256,256]{1,0:T(8,128)(2,1)S(1)} %all_gather.22) | copy-start | bytes 393220
  233.2 69.4 %copy-start.10 = (pred[32,256]{1,0:T(8,128)(4,1)}, pred[32,256]{1,0:T(8,128)(4,1)S(1)}, u32[]{:S(2)}) copy-start(pred[32,256]{1,0:T(8,128)(4,1)S(1)} %compare_and_fusion) | copy-start | bytes 24580
  331.4 5.7 %copy-start.14 = (s32[4]{0:T(128)S(1)}, s32[4]{0:T(128)}, u32[]{:S(2)}) copy-start(s32[4]{0:T(128)} %param.27) | copy-start | bytes 52
  331.4 5.7 %copy-start.15 = (s32[4,8]{1,0:T(4,128)S(1)}, s32[4,8]{1,0:T(4,128)}, u32[]{:S(2)}) copy-start(s32[4,8]{1,0:T(4,128)} %param.30) | copy-start | bytes 388
  331.4 6.6 %copy-start.9 = (bf16[256,256]{1,0:T(8,128)(2,1)S(1)}, bf16[256,256]{1,0:T(8,128)(2,1)}, u32[]{:S(2)}) copy-start(bf16[256,256]{1,0:T(8,128)(2,1)} %copy-done.8) | copy-start | bytes 393220
  344.9 10.6 %copy-start = (bf16[4,1024,256]{2,1,0:T(8,128)(2,1)}, bf16[4,1024,256]{2,1,0:T(8,128)(2,1)S(1)}, u32[]{:S(2)}) copy-start(bf16[4,1024,256]{2,1,0:T(8,128)(2,1)S(1)} %scatter_fusion.2) | copy-start | bytes 6291460
Sparse Core Ops, SparseCore 0:
  167.6 74.6 all-gather.1
  337.2 18.2 reduce-scatter.1
